TPU v7x, 512 devices: a whole 4x4x16 slice. The times are simulated.
512 devices in a mesh: segment: 8 (over x, core), dp: 64 (over y, z).
Axes of the slice: x: 4, y: 4, z: 16, core: 2. Of those that a mesh axis runs over, the one named last changes fastest.
Arguments:
- hidden: bfloat16 [8, 8192, 8192], P('segment', 'dp'), may hold values from -6 to 6
- store_a: bfloat16 [8, 32, 64, 8192], P('segment', None, None, 'dp'), may hold values from -0.0625 to 0.0625
- store_b: bfloat16 [8, 32, 64, 8192], P('segment', None, None, 'dp'), may hold values from -0.75 to 0.75
- request_start: int32 [8, 32], P('segment'), may hold values from 0 to 8128, as said below
- request_adapter: int32 [8, 32], P('segment'), may hold values from 0 to 31
Outputs:
- updated: bfloat16 [8, 8192, 8192], P('segment', 'dp')
Inputs may be any that keep to these rules, and one draw needn't show every extreme that they name: `request_start`: in each group the starts rise strictly from 0, are multiples of 64, and the last is 8128.
All inputs are finite; a program needn't handle non-finite values.
Results may differ from a plain program's by a relative error of at most 0.006.
Values may be sent and summed in bfloat16 or wider, within the bound.
No kernel may reach another device: no remote copies, remote signals or barrier semaphores. Data moves between devices by JAX's collectives and lax.ppermute only.
A program may use at most 64 MiB of HBM per device.

v0:
```python
import jax
import jax.numpy as jnp
from jax import lax
from jax.sharding import PartitionSpec as P

BLOCK = 64
STEPS = 2
EPS = 1e-05
ADAPTER_SCALE = 0.5


def from_behind(block, axis, distance):
    devices = range(lax.axis_size(axis))
    route = [((i - distance) % len(devices), i) for i in devices]
    return lax.ppermute(block, axis, route)


def block_adapters(starts, adapters, total_rows):
    blocks = total_rows // BLOCK
    block_start = jnp.arange(blocks, dtype=jnp.int32) * BLOCK
    request = jnp.sum((starts[None, :] <= block_start[:, None]).astype(jnp.int32), axis=1) - 1
    labels = jnp.arange(adapters.shape[0], dtype=jnp.int32)
    picked = jnp.where(request[:, None] == labels[None, :], adapters[None, :], 0)
    return jnp.sum(picked, axis=1)


def apply_layer(state, starts, adapters, slice_a, slice_b):
    value_rows = state.astype(jnp.float32)
    meansq = jnp.mean(value_rows * value_rows, axis=-1, keepdims=True)
    normed = (value_rows * lax.rsqrt(meansq + EPS)).astype(jnp.bfloat16)
    rank_width = slice_a.shape[1]
    columns = lax.all_to_all(normed, "dp", split_axis=1, concat_axis=0, tiled=True)
    total_rows, width = columns.shape
    blocks = total_rows // BLOCK
    chosen = block_adapters(starts, adapters, total_rows)
    down = jnp.take(slice_a, chosen, axis=0)
    grouped = columns.reshape(blocks, BLOCK, width)
    partial_rank = jnp.einsum("bic,brc->bir", grouped, down, preferred_element_type=jnp.float32)
    partial_rank = partial_rank.reshape(total_rows, rank_width)
    rank = lax.psum(partial_rank, "dp").astype(jnp.bfloat16)
    upper = jnp.take(slice_b, chosen, axis=0)
    adapter_update = jnp.einsum(
        "bir,brc->bic",
        rank.reshape(blocks, BLOCK, rank_width),
        upper,
        preferred_element_type=jnp.float32,
    )
    adapter_update = adapter_update.reshape(total_rows, width).astype(jnp.bfloat16)
    returned_rows = lax.all_to_all(adapter_update, "dp", split_axis=0, concat_axis=1, tiled=True)
    return (value_rows + ADAPTER_SCALE * returned_rows.astype(jnp.float32)).astype(jnp.bfloat16)


def shards(hidden, store_a, store_b, request_start, request_adapter):
    state = hidden[0]
    starts = request_start[0]
    adapters = request_adapter[0]
    slice_a = store_a[0]
    slice_b = store_b[0]
    for step in range(STEPS):
        if step > 0:
            state = from_behind(state, "segment", 1)
            starts, adapters = from_behind((starts, adapters), "segment", 1)
        state = apply_layer(state, starts, adapters, slice_a, slice_b)
    state = from_behind(state, "segment", 1 - STEPS)
    return state[None]


def solution(mesh):
    return jax.shard_map(
        shards,
        mesh=mesh,
        in_specs=(
            P("segment", "dp", None),
            P("segment", None, None, "dp"),
            P("segment", None, None, "dp"),
            P("segment", None),
            P("segment", None),
        ),
        out_specs=P("segment", "dp", None),
        check_vma=False,
    )
```

profile of v0, /device:TPU:45, one launch (start us, length us, event | category | flops | bytes accessed | tf_op | source)
XLA Modules:
  0.0 1126.6 jit_solution(4705812348207641893)
XLA Ops:
  0.0 2.2 convert_bitcast_fusion
  3.5 3.8 fusion.7
  7.3 18.0 %all-to-all-start = ((bf16[128,64,128]{2,0,1:T(8,128)(2,1)}), bf16[128,64,128]{2,0,1:T(8,128)(2,1)}, u32[]{:S(2)}, u32[]{:S(2)}) async-start(bf16[128,64,128]{2,0,1:T(8,128)(2,1)} %fusion.7), calls=%async_computation | async-start | bytes 4194304 | tf_op jit(solution)/shard_map/all_to_all | solution.py:32
  25.4 2.0 collective-permute-start.1
  28.4 2.2 gather_fusion
  30.6 2.1 gather_fusion.1
  32.7 89.3 %all-to-all-done = bf16[128,64,128]{2,0,1:T(8,128)(2,1)} async-done(((bf16[128,64,128]{2,0,1:T(8,128)(2,1)}), bf16[128,64,128]{2,0,1:T(8,128)(2,1)}, u32[]{:S(2)}, u32[]{:S(2)}) %all-to-all-start) | async-done | bytes 2097184 | tf_op jit(solution)/shard_map/all_to_all | solution.py:32
  122.1 5.4 fusion.15
  127.5 248.0 %all-reduce.2 = bf16[8192,64]{1,0:T(8,128)(2,1)} all-reduce(f32[8192,64]{1,0:T(8,128)} %bitcast.57), channel_id=1, replica_groups=mesh['segment'=8,'dp'=64] {'dp'}, use_global_device_ids=true, to_apply=%region_3.5 | all-reduce | flops 524288 | bytes 3145728 | tf_op jit(solution)/shard_map/psum | solution.py:40
  375.5 3.0 fusion.21
  378.5 82.6 %all_to_all.49 = bf16[64,128,128]{2,1,0:T(8,128)(2,1)S(1)} all-to-all(bf16[64,128,128]{2,1,0:T(8,128)(2,1)S(1)} %bitcast.61), channel_id=1, replica_groups=mesh['segment'=8,'dp'=64] {'dp'}, dimensions={0} | all-to-all | bytes 4194304 | tf_op jit(solution)/shard_map/all_to_all | solution.py:49
  461.7 84.9 %collective-permute-start = (bf16[128,8192]{1,0:T(8,128)(2,1)S(1)}, bf16[128,8192]{1,0:T(8,128)(2,1)S(1)}, u32[]{:S(2)}, u32[]{:S(2)}) collective-permute-start(bf16[128,8192]{1,0:T(8,128)(2,1)S(1)} %fusion.3), channel_id=1, source_target_pairs={{448,0},{0,64},{64,128},{128,192},{192,256},{256,320},{320,384},{3... | collective-permute-start | bytes 6291464 | tf_op jit(solution)/shard_map/ppermute | solution.py:15
  546.6 23.0 %collective-permute-done = bf16[128,8192]{1,0:T(8,128)(2,1)S(1)} collective-permute-done((bf16[128,8192]{1,0:T(8,128)(2,1)S(1)}, bf16[128,8192]{1,0:T(8,128)(2,1)S(1)}, u32[]{:S(2)}, u32[]{:S(2)}) %collective-permute-start) | collective-permute-done | bytes 2097184 | tf_op jit(solution)/shard_map/ppermute | solution.py:15
  572.0 7.3 all-to-all-start.2
  579.3 3.1 collective-permute-start.2
  583.2 2.2 gather_fusion.2
  585.4 2.1 gather_fusion.3
  587.6 87.6 %all-to-all-done.2 = bf16[128,64,128]{2,0,1:T(8,128)(2,1)} async-done(((bf16[128,64,128]{2,0,1:T(8,128)(2,1)}), bf16[128,64,128]{2,0,1:T(8,128)(2,1)}, u32[]{:S(2)}, u32[]{:S(2)}) %all-to-all-start.2) | async-done | bytes 2097184 | tf_op jit(solution)/shard_map/all_to_all | solution.py:32
  675.2 5.4 fusion.11
  680.7 246.4 %all-reduce.3 = bf16[8192,64]{1,0:T(8,128)(2,1)} all-reduce(f32[8192,64]{1,0:T(8,128)} %bitcast.58), channel_id=1, replica_groups=mesh['segment'=8,'dp'=64] {'dp'}, use_global_device_ids=true, to_apply=%region_7.9 | all-reduce | flops 524288 | bytes 3145728 | tf_op jit(solution)/shard_map/psum | solution.py:40
  927.0 3.0 fusion.24
  930.0 83.2 %all_to_all.50 = bf16[64,128,128]{2,1,0:T(8,128)(2,1)S(1)} all-to-all(bf16[64,128,128]{2,1,0:T(8,128)(2,1)S(1)} %bitcast.62), channel_id=1, replica_groups=mesh['segment'=8,'dp'=64] {'dp'}, dimensions={0} | all-to-all | bytes 4194304 | tf_op jit(solution)/shard_map/all_to_all | solution.py:49
  1013.9 84.6 %collective-permute-start.3 = (bf16[128,8192]{1,0:T(8,128)(2,1)S(1)}, bf16[128,8192]{1,0:T(8,128)(2,1)S(1)}, u32[]{:S(2)}, u32[]{:S(2)}) collective-permute-start(bf16[128,8192]{1,0:T(8,128)(2,1)S(1)} %fusion.6), channel_id=1, source_target_pairs={{64,0},{128,64},{192,128},{256,192},{320,256},{384,320},{448,384},... | collective-permute-start | bytes 6291464 | tf_op jit(solution)/shard_map/ppermute | solution.py:15
  1098.5 26.9 %collective-permute-done.3 = bf16[128,8192]{1,0:T(8,128)(2,1)S(1)} collective-permute-done((bf16[128,8192]{1,0:T(8,128)(2,1)S(1)}, bf16[128,8192]{1,0:T(8,128)(2,1)S(1)}, u32[]{:S(2)}, u32[]{:S(2)}) %collective-permute-start.3) | collective-permute-done | bytes 2097184 | tf_op jit(solution)/shard_map/ppermute | solution.py:15
  (33 shorter events, 8.2 us)
Async XLA Ops:
  0.0 28.3 %copy-start = (bf16[1,32,64,128]{3,2,1,0:T(8,128)(2,1)S(1)}, bf16[1,32,64,128]{3,2,1,0:T(8,128)(2,1)}, u32[]{:S(2)}) copy-start(bf16[1,32,64,128]{3,2,1,0:T(8,128)(2,1)} %param.8) | copy-start | bytes 1572868
  0.0 2.3 copy-start.2
  7.3 18.1 %copy-start.3 = (s32[1,32]{1,0:T(1,128)S(1)}, s32[1,32]{1,0:T(1,128)}, u32[]{:S(2)}) copy-start(s32[1,32]{1,0:T(1,128)} %param.10) | copy-start | bytes 388
  7.3 20.9 %copy-start.4 = (s32[1,32]{1,0:T(1,128)S(1)}, s32[1,32]{1,0:T(1,128)}, u32[]{:S(2)}) copy-start(s32[1,32]{1,0:T(1,128)} %param.11) | copy-start | bytes 388
  7.3 114.8 %all-to-all-start = ((bf16[128,64,128]{2,0,1:T(8,128)(2,1)}), bf16[128,64,128]{2,0,1:T(8,128)(2,1)}, u32[]{:S(2)}, u32[]{:S(2)}) async-start(bf16[128,64,128]{2,0,1:T(8,128)(2,1)} %fusion.7), calls=%async_computation | async-start | bytes 4194304 | tf_op jit(solution)/shard_map/all_to_all | solution.py:32
  25.4 2.8 collective-permute-start.1
  28.3 2.2 copy-start.1
  461.7 107.9 %collective-permute-start = (bf16[128,8192]{1,0:T(8,128)(2,1)S(1)}, bf16[128,8192]{1,0:T(8,128)(2,1)S(1)}, u32[]{:S(2)}, u32[]{:S(2)}) collective-permute-start(bf16[128,8192]{1,0:T(8,128)(2,1)S(1)} %fusion.3), channel_id=1, source_target_pairs={{448,0},{0,64},{64,128},{128,192},{192,256},{256,320},{320,384},{3... | collective-permute-start | bytes 6291464 | tf_op jit(solution)/shard_map/ppermute | solution.py:15
  572.0 103.2 %all-to-all-start.2 = ((bf16[128,64,128]{2,0,1:T(8,128)(2,1)}), bf16[128,64,128]{2,0,1:T(8,128)(2,1)}, u32[]{:S(2)}, u32[]{:S(2)}) async-start(bf16[128,64,128]{2,0,1:T(8,128)(2,1)} %copy_bitcast_fusion), calls=%async_computation.2 | async-start | bytes 4194304 | tf_op jit(solution)/shard_map/all_to_all | solution.py:32
  579.3 3.8 collective-permute-start.2
  1013.9 111.4 %collective-permute-start.3 = (bf16[128,8192]{1,0:T(8,128)(2,1)S(1)}, bf16[128,8192]{1,0:T(8,128)(2,1)S(1)}, u32[]{:S(2)}, u32[]{:S(2)}) collective-permute-start(bf16[128,8192]{1,0:T(8,128)(2,1)S(1)} %fusion.6), channel_id=1, source_target_pairs={{64,0},{128,64},{192,128},{256,192},{320,256},{384,320},{448,384},... | collective-permute-start | bytes 6291464 | tf_op jit(solution)/shard_map/ppermute | solution.py:15
where the time goes:
time: 1130 us
  blocking collectives  660 us (58%)
  waiting for transfers between devices  228 us (20%)
  starting transfers between devices  200 us (18%)
  matrix products  16.9 us (1%)
    psum x2, blocking collectives, apply_layer(): rank = lax.psum(partial_rank, 'dp').astype(jnp.bfloat16)  494 us
    all_to_all x2, waiting for transfers between devices, apply_layer(): lax.all_to_all(normed, 'dp', split_axis=1, concat_axis=0, tiled=True)  177 us
    ppermute x4, starting transfers between devices, from_behind(): return lax.ppermute(block, axis, route)  175 us
    all_to_all x2, blocking collectives, apply_layer(): lax.all_to_all(adapter_update, 'dp', split_axis=0, concat_axis=1, tiled=T...  166 us
    ppermute x4, waiting for transfers between devices, from_behind(): return lax.ppermute(block, axis, route)  51.3 us
    all_to_all x2, starting transfers between devices, apply_layer(): lax.all_to_all(normed, 'dp', split_axis=1, concat_axis=0, tiled=True)  25.4 us
  transfers between devices with their start and end apart: 6, of which 6 were waited for; matrix products, arithmetic and copies ran while one was open for 1% of the time, Pallas kernels for 0%

commit v1 on v0

--- a/solution.py
+++ b/solution.py
@@ -29,7 +29,10 @@
     meansq = jnp.mean(value_rows * value_rows, axis=-1, keepdims=True)
     normed = (value_rows * lax.rsqrt(meansq + EPS)).astype(jnp.bfloat16)
     rank_width = slice_a.shape[1]
-    columns = lax.all_to_all(normed, "dp", split_axis=1, concat_axis=0, tiled=True)
+    main = jax.lax.all_to_all(
+        jnp.stack(jnp.split(normed, jax.lax.axis_size("dp"), 1), 0), "dp", 0, 0
+    )
+    columns = jnp.concatenate(main, 0)
     total_rows, width = columns.shape
     blocks = total_rows // BLOCK
     chosen = block_adapters(starts, adapters, total_rows)

time: 1130 us -> 1200 us (1.062)
  the two profiles are of different devices: /device:TPU:45 before, /device:TPU:1 now
where the time goes in v1:
time: 1200 us
  blocking collectives  668 us (56%)
  waiting for transfers between devices  219 us (18%)
  starting transfers between devices  200 us (17%)
  local copies, waits for them, and re-layouts  90 us (8%)
  matrix products  16.9 us (1%)
    psum x2, blocking collectives, apply_layer(): rank = lax.psum(partial_rank, 'dp').astype(jnp.bfloat16)  554 us
    ppermute x4, starting transfers between devices, from_behind(): return lax.ppermute(block, axis, route)  172 us
    all_to_all x2, waiting for transfers between devices, apply_layer(): jax.lax.all_to_all(jnp.stack(jnp.split(normed, jax.lax.axis_size('dp'), 1...  170 us
    all_to_all x2, blocking collectives, apply_layer(): lax.all_to_all(adapter_update, 'dp', split_axis=0, concat_axis=1, tiled=T...  114 us
    unnamed x137, local copies, waits for them, and re-layouts  80 us
    ppermute x4, waiting for transfers between devices, from_behind(): return lax.ppermute(block, axis, route)  48.4 us
    all_to_all x2, starting transfers between devices, apply_layer(): jax.lax.all_to_all(jnp.stack(jnp.split(normed, jax.lax.axis_size('dp'), 1...  28.6 us
  transfers between devices with their start and end apart: 6, of which 6 were waited for; matrix products, arithmetic and copies ran while one was open for 1% of the time, Pallas kernels for 0%

profile of v1, /device:TPU:1, one launch (start us, length us, event | category | flops | bytes accessed | tf_op | source)
XLA Modules:
  0.0 1199.3 jit_solution(10479302093871429923)
XLA Ops:
  0.0 2.2 fusion.3
  42.7 19.7 %all-to-all-start = ((bf16[64,128,128]{2,1,0:T(8,128)(2,1)}), bf16[64,128,128]{2,1,0:T(8,128)(2,1)}, u32[]{:S(2)}, u32[]{:S(2)}) async-start(bf16[64,128,128]{2,1,0:T(8,128)(2,1)} %constant_dynamic-update-slice_fusion), calls=%async_computation | async-start | bytes 4194304 | tf_op jit(solution)/shard_map/all_to_all | solution.py:32
  62.4 2.1 collective-permute-start.1
  65.4 2.2 gather_fusion
  67.6 2.1 gather_fusion.1
  69.8 87.3 %all-to-all-done = bf16[64,128,128]{2,1,0:T(8,128)(2,1)} async-done(((bf16[64,128,128]{2,1,0:T(8,128)(2,1)}), bf16[64,128,128]{2,1,0:T(8,128)(2,1)}, u32[]{:S(2)}, u32[]{:S(2)}) %all-to-all-start) | async-done | bytes 2097184 | tf_op jit(solution)/shard_map/all_to_all | solution.py:32
  157.1 5.4 fusion.12
  162.5 275.2 %all-reduce.2 = bf16[8192,64]{1,0:T(8,128)(2,1)} all-reduce(f32[8192,64]{1,0:T(8,128)} %bitcast.550), channel_id=1, replica_groups=mesh['segment'=8,'dp'=64] {'dp'}, use_global_device_ids=true, to_apply=%region_3.5 | all-reduce | flops 524288 | bytes 3145728 | tf_op jit(solution)/shard_map/psum | solution.py:43
  437.7 3.0 fusion.18
  440.7 57.8 %all_to_all.30 = bf16[64,128,128]{2,1,0:T(8,128)(2,1)S(1)} all-to-all(bf16[64,128,128]{2,1,0:T(8,128)(2,1)S(1)} %bitcast.554), channel_id=1, replica_groups=mesh['segment'=8,'dp'=64] {'dp'}, dimensions={0} | all-to-all | bytes 4194304 | tf_op jit(solution)/shard_map/all_to_all | solution.py:52
  499.2 83.1 %collective-permute-start = (bf16[128,8192]{1,0:T(8,128)(2,1)S(1)}, bf16[128,8192]{1,0:T(8,128)(2,1)S(1)}, u32[]{:S(2)}, u32[]{:S(2)}) collective-permute-start(bf16[128,8192]{1,0:T(8,128)(2,1)S(1)} %fusion.5), channel_id=1, source_target_pairs={{448,0},{0,64},{64,128},{128,192},{192,256},{256,320},{320,384},{3... | collective-permute-start | bytes 6291464 | tf_op jit(solution)/shard_map/ppermute | solution.py:15
  582.2 23.0 %collective-permute-done = bf16[128,8192]{1,0:T(8,128)(2,1)S(1)} collective-permute-done((bf16[128,8192]{1,0:T(8,128)(2,1)S(1)}, bf16[128,8192]{1,0:T(8,128)(2,1)S(1)}, u32[]{:S(2)}, u32[]{:S(2)}) %collective-permute-start) | collective-permute-done | bytes 2097184 | tf_op jit(solution)/shard_map/ppermute | solution.py:15
  646.2 8.9 all-to-all-start.2
  655.1 2.8 collective-permute-start.2
  658.9 2.2 gather_fusion.2
  661.1 2.1 gather_fusion.3
  663.3 83.0 %all-to-all-done.2 = bf16[64,128,128]{2,1,0:T(8,128)(2,1)} async-done(((bf16[64,128,128]{2,1,0:T(8,128)(2,1)}), bf16[64,128,128]{2,1,0:T(8,128)(2,1)}, u32[]{:S(2)}, u32[]{:S(2)}) %all-to-all-start.2) | async-done | bytes 2097184 | tf_op jit(solution)/shard_map/all_to_all | solution.py:32
  746.3 5.4 fusion.8
  751.8 279.1 %all-reduce.3 = bf16[8192,64]{1,0:T(8,128)(2,1)} all-reduce(f32[8192,64]{1,0:T(8,128)} %bitcast.551), channel_id=1, replica_groups=mesh['segment'=8,'dp'=64] {'dp'}, use_global_device_ids=true, to_apply=%region_7.9 | all-reduce | flops 524288 | bytes 3145728 | tf_op jit(solution)/shard_map/psum | solution.py:43
  1030.9 3.0 fusion.21
  1033.9 55.8 %all_to_all.31 = bf16[64,128,128]{2,1,0:T(8,128)(2,1)S(1)} all-to-all(bf16[64,128,128]{2,1,0:T(8,128)(2,1)S(1)} %bitcast.555), channel_id=1, replica_groups=mesh['segment'=8,'dp'=64] {'dp'}, dimensions={0} | all-to-all | bytes 4194304 | tf_op jit(solution)/shard_map/all_to_all | solution.py:52
  1090.3 84.0 %collective-permute-start.3 = (bf16[128,8192]{1,0:T(8,128)(2,1)S(1)}, bf16[128,8192]{1,0:T(8,128)(2,1)S(1)}, u32[]{:S(2)}, u32[]{:S(2)}) collective-permute-start(bf16[128,8192]{1,0:T(8,128)(2,1)S(1)} %fusion.2), channel_id=1, source_target_pairs={{64,0},{128,64},{192,128},{256,192},{320,256},{384,320},{448,384},... | collective-permute-start | bytes 6291464 | tf_op jit(solution)/shard_map/ppermute | solution.py:15
  1174.3 23.8 %collective-permute-done.3 = bf16[128,8192]{1,0:T(8,128)(2,1)S(1)} collective-permute-done((bf16[128,8192]{1,0:T(8,128)(2,1)S(1)}, bf16[128,8192]{1,0:T(8,128)(2,1)S(1)}, u32[]{:S(2)}, u32[]{:S(2)}) %collective-permute-start.3) | collective-permute-done | bytes 2097184 | tf_op jit(solution)/shard_map/ppermute | solution.py:15
  1198.0 1.3 copy.145
  (159 shorter events, 84.7 us)
Async XLA Ops:
  0.0 65.4 %copy-start = (bf16[1,32,64,128]{3,2,1,0:T(8,128)(2,1)S(1)}, bf16[1,32,64,128]{3,2,1,0:T(8,128)(2,1)}, u32[]{:S(2)}) copy-start(bf16[1,32,64,128]{3,2,1,0:T(8,128)(2,1)} %param.8) | copy-start | bytes 1572868
  0.0 2.3 copy-start.2
  42.7 19.7 %copy-start.3 = (s32[1,32]{1,0:T(1,128)S(1)}, s32[1,32]{1,0:T(1,128)}, u32[]{:S(2)}) copy-start(s32[1,32]{1,0:T(1,128)} %param.10) | copy-start | bytes 388
  42.7 22.6 %copy-start.4 = (s32[1,32]{1,0:T(1,128)S(1)}, s32[1,32]{1,0:T(1,128)}, u32[]{:S(2)}) copy-start(s32[1,32]{1,0:T(1,128)} %param.11) | copy-start | bytes 388
  42.7 114.4 %all-to-all-start = ((bf16[64,128,128]{2,1,0:T(8,128)(2,1)}), bf16[64,128,128]{2,1,0:T(8,128)(2,1)}, u32[]{:S(2)}, u32[]{:S(2)}) async-start(bf16[64,128,128]{2,1,0:T(8,128)(2,1)} %constant_dynamic-update-slice_fusion), calls=%async_computation | async-start | bytes 4194304 | tf_op jit(solution)/shard_map/all_to_all | solution.py:32
  62.4 2.8 collective-permute-start.1
  65.4 2.2 copy-start.1
  499.2 106.0 %collective-permute-start = (bf16[128,8192]{1,0:T(8,128)(2,1)S(1)}, bf16[128,8192]{1,0:T(8,128)(2,1)S(1)}, u32[]{:S(2)}, u32[]{:S(2)}) collective-permute-start(bf16[128,8192]{1,0:T(8,128)(2,1)S(1)} %fusion.5), channel_id=1, source_target_pairs={{448,0},{0,64},{64,128},{128,192},{192,256},{256,320},{320,384},{3... | collective-permute-start | bytes 6291464 | tf_op jit(solution)/shard_map/ppermute | solution.py:15
  646.2 100.2 %all-to-all-start.2 = ((bf16[64,128,128]{2,1,0:T(8,128)(2,1)}), bf16[64,128,128]{2,1,0:T(8,128)(2,1)}, u32[]{:S(2)}, u32[]{:S(2)}) async-start(bf16[64,128,128]{2,1,0:T(8,128)(2,1)} %constant_dynamic-update-slice_fusion.64), calls=%async_computation.2 | async-start | bytes 4194304 | tf_op jit(solution)/shard_map/all_to_all | solution.py:32
  655.1 3.8 collective-permute-start.2
  1090.3 107.8 %collective-permute-start.3 = (bf16[128,8192]{1,0:T(8,128)(2,1)S(1)}, bf16[128,8192]{1,0:T(8,128)(2,1)S(1)}, u32[]{:S(2)}, u32[]{:S(2)}) collective-permute-start(bf16[128,8192]{1,0:T(8,128)(2,1)S(1)} %fusion.2), channel_id=1, source_target_pairs={{64,0},{128,64},{192,128},{256,192},{320,256},{384,320},{448,384},... | collective-permute-start | bytes 6291464 | tf_op jit(solution)/shard_map/ppermute | solution.py:15
